TPU v7x, 256 devices: a whole 4x4x8 slice. The times are simulated.
256 devices in a mesh: row: 16 (over y, x), col: 16 (over z, core).
Axes of the slice: x: 4, y: 4, z: 8, core: 2. Of those that a mesh axis runs over, the one named last changes fastest.
Arguments:
- factor_diag: float32 [2, 512, 512], replicated, as said below
- factor_mid: float32 [512, 512], replicated, may hold values from -0.25 to 0.25
- factor_low: float32 [2, 16384, 512], P(None, ('row', 'col')), may hold values from -0.046875 to 0.046875
- adjoint_diag: float32 [2, 512, 512], replicated, may hold values from -6 to 6
- adjoint_mid: float32 [512, 512], replicated, may hold values from -6 to 6
- adjoint_low: float32 [2, 16384, 512], P(None, ('row', 'col')), may hold values from -6 to 6
- trailing_adjoint: float32 [16384, 16, 1024], P('row', None, 'col'), as said below
Outputs:
- grad_diag: float32 [2, 512, 512], replicated
- grad_mid: float32 [512, 512], replicated
- grad_low: float32 [2, 16384, 512], P(None, ('row', 'col'))
Inputs may be any that keep to these rules, and one draw needn't show every extreme that they name: `factor_diag`: each of the two [512, 512] blocks is lower triangular with diagonal entries between 1 and 2. `trailing_adjoint`: symmetric when read as an 16384 x 16384 matrix in row-major order.
All inputs are finite; a program needn't handle non-finite values.
Results may differ from a plain program's by a relative error of at most 0.000065.
Values sent between devices are 32-bit elements; how exact they have to be, the bound alone decides.
No kernel may reach another device: no remote copies, remote signals or barrier semaphores. Data moves between devices by JAX's collectives and lax.ppermute only.
A program may use at most 128 MiB of HBM per device.

v0:
```python
import jax
import jax.numpy as jnp
from jax import lax
from jax.sharding import PartitionSpec as P


def lower_half(matrix):
    return jnp.tril(matrix, -1) + 0.5 * jnp.diag(jnp.diag(matrix))


def product(left_side, right_side):
    return jnp.dot(
        left_side, right_side, precision=lax.Precision.HIGHEST, preferred_element_type=jnp.float32
    )


def right_solve(factor, row_block):
    return jax.scipy.linalg.solve_triangular(factor, row_block.T, trans=1, lower=True).T


def diag_adjoint(factor, adjoint):
    inner_term = lower_half(product(factor.T, adjoint))
    halfway = jax.scipy.linalg.solve_triangular(factor, inner_term, trans=1, lower=True)
    whole_term = right_solve(factor, halfway)
    return 0.5 * (whole_term + whole_term.T)


def shards(
    factor_diag, factor_mid, factor_low, adjoint_diag, adjoint_mid, adjoint_low, trailing_adjoint
):
    block_rows, row_groups, group_cols = trailing_adjoint.shape
    local_block = trailing_adjoint.reshape(block_rows, row_groups * group_cols)

    def image_of(panel):
        columns = lax.all_gather(panel, "row", axis=0, tiled=True)
        return lax.psum_scatter(
            product(local_block, columns), "col", scatter_dimension=0, tiled=True
        )

    second_image = image_of(factor_low[1])
    first_image = image_of(factor_low[0])
    second_solved = right_solve(factor_diag[1], adjoint_low[1] - 2.0 * second_image)
    second_total = lax.psum(product(second_solved.T, factor_low[1]), ("row", "col"))
    second_grad = diag_adjoint(factor_diag[1], adjoint_diag[1] - second_total)
    second_half = 0.5 * second_solved
    upper_term = product(second_half.T, factor_low[0])
    bottom_rows = adjoint_low[0] - 2.0 * (product(second_half, factor_mid) + first_image)
    bottom_solved = right_solve(factor_diag[0], bottom_rows)
    lower_term = product(bottom_solved.T, factor_low[0])
    upper_total = lax.psum(upper_term, ("row", "col"))
    lower_total = lax.psum(lower_term, ("row", "col"))
    top_rows = adjoint_mid - 2.0 * (product(second_grad, factor_mid) + upper_total)
    top_solved = right_solve(factor_diag[0], top_rows)
    first_adjoint = adjoint_diag[0] - product(top_solved.T, factor_mid) - lower_total
    first_grad = diag_adjoint(factor_diag[0], first_adjoint)
    return (
        jnp.stack([first_grad, second_grad]),
        0.5 * top_solved,
        jnp.stack([0.5 * bottom_solved, second_half]),
    )


def solution(mesh):
    return jax.shard_map(
        shards,
        mesh=mesh,
        in_specs=(
            P(),
            P(),
            P(None, ("row", "col"), None),
            P(),
            P(),
            P(None, ("row", "col"), None),
            P("row", None, "col"),
        ),
        out_specs=(P(), P(), P(None, ("row", "col"), None)),
        check_vma=False,
    )
```

profile of v0, /device:TPU:2, one launch (start us, length us, event | category | flops | bytes accessed | tf_op | source)
XLA Modules:
  0.0 587.7 jit_solution(3043104510383694873)
XLA Ops:
  7.2 1.8 fusion.165
  9.1 0.7 all-gather.7.cloned.1.call-update
  9.8 53.8 %all-gather.5.cloned.1.call-done = f32[1,1024,512]{2,1,0:T(8,128)} async-done(((f32[1,64,512]{2,1,0:T(8,128)}), f32[1,1024,512]{2,1,0:T(8,128)}) %all-gather.5.cloned.1.call-update) | async-done | bytes 2097168 | tf_op jit(solution)/shard_map/all_gather | solution.py:35
  63.6 10.2 %fusion.2 = f32[1024,512]{1,0:T(8,128)} fusion(f32[1024,1024]{0,1:T(8,128)} %bitcast.202, f32[1,1024,512]{2,1,0:T(8,128)} %all-gather.5.cloned.1.call-done), kind=kOutput, calls=%fused_computation.9 | convolution fusion | flops 6442450944 | bytes 8388608 | tf_op jit(solution)/shard_map/dot_general | solution.py:12
  73.8 1.5 copy-done.1
  75.3 1.6 bitcast_select_fusion.1
  76.9 39.0 %all-gather.7.cloned.1.call-done = f32[1,1024,512]{2,1,0:T(8,128)} async-done(((f32[1,64,512]{2,1,0:T(8,128)}), f32[1,1024,512]{2,1,0:T(8,128)}) %all-gather.7.cloned.1.call-update) | async-done | bytes 2097168 | tf_op jit(solution)/shard_map/all_gather | solution.py:35
  115.9 10.2 %fusion = f32[1024,512]{1,0:T(8,128)} fusion(f32[1024,1024]{0,1:T(8,128)} %bitcast.203, f32[1,1024,512]{2,1,0:T(8,128)} %all-gather.7.cloned.1.call-done), kind=kOutput, calls=%fused_computation.7 | convolution fusion | flops 6442450944 | bytes 8388608 | tf_op jit(solution)/shard_map/dot_general | solution.py:12
  126.4 12.0 %while.14 = (s32[]{:T(128)}, f32[512,512]{1,0:T(8,128)}, s32[4,2]{0,1:T(2,128)S(1)}, f32[4,128,128]{2,1,0:T(8,128)S(1)}, s32[]{:T(128)}) while((s32[]{:T(128)}, f32[512,512]{1,0:T(8,128)}, s32[4,2]{0,1:T(2,128)S(1)}, f32[4,128,128]{2,1,0:T(8,128)S(1)}, s32[]{:T(128)}) %tuple.62), condition=%wide.while_cond.1.clone, body=%wide.while_body.1.clone.sunk | while | flops 2 | bytes 131181 | solution.py:18
  127.1 2.3 bitcast_dynamic-update-slice_fusion.4
  130.1 2.3 bitcast_dynamic-update-slice_fusion.4
  133.1 2.3 bitcast_dynamic-update-slice_fusion.4
  136.2 2.3 bitcast_dynamic-update-slice_fusion.4
  138.5 39.3 %custom-call.17 = f32[4,128,128]{1,2,0:T(8,128)S(1)} custom-call(f32[4,128,128]{2,1,0:T(8,128)S(1)} %get-tuple-element.53), custom_call_target="InvertDiagBlocksLowerTriangular" | custom-call | tf_op jit(solution)/shard_map/jit(_solve_triangular)/triangular_solve | solution.py:18
  177.8 7.7 %while.15 = (s32[]{:T(128)}, f32[512,512]{1,0:T(8,128)S(1)}, s32[4,2]{0,1:T(2,128)S(1)}, f32[4,128,128]{2,1,0:T(8,128)S(1)}, s32[]{:T(128)}) while((s32[]{:T(128)}, f32[512,512]{1,0:T(8,128)S(1)}, s32[4,2]{0,1:T(2,128)S(1)}, f32[4,128,128]{2,1,0:T(8,128)S(1)}, s32[]{:T(128)}) %tuple.80), condition=%wide.while_cond.1.clone.3, body=%wide.while_body.1.clone.3.sunk | while | flops 2 | bytes 131181 | solution.py:18
  178.4 1.3 bitcast_dynamic-update-slice_fusion.5
  180.4 1.3 bitcast_dynamic-update-slice_fusion.5
  182.3 1.3 bitcast_dynamic-update-slice_fusion.5
  184.2 1.3 bitcast_dynamic-update-slice_fusion.5
  185.5 0.7 copy-done.21
  186.2 40.1 %custom-call.21 = f32[4,128,128]{1,2,0:T(8,128)S(1)} custom-call(f32[4,128,128]{2,1,0:T(8,128)} %copy-done.21), custom_call_target="InvertDiagBlocksLowerTriangular" | custom-call | tf_op jit(solution)/shard_map/jit(_solve_triangular)/triangular_solve | solution.py:18
  226.4 1.0 fusion.81
  227.6 1.0 convolution_subtract_fusion.21
  228.9 1.1 convolution_subtract_fusion.20
  230.3 1.2 convolution_subtract_fusion.19
  231.7 2.0 fusion.77
  233.8 2.0 fusion.79
  235.8 5.0 reduce-scatter.5.cloned.1.call-done
  240.7 1.7 fusion.10
  244.1 2.0 fusion.75
  246.3 0.7 pad_maximum_fusion.5
  247.0 265.8 %all-reduce.3.cloned.1.call-done = (f32[512,512]{1,0:T(8,128)}, f32[512,512]{1,0:T(8,128)}, f32[512,512]{1,0:T(8,128)}) async-done(((f32[512,512]{1,0:T(8,128)}, f32[512,512]{1,0:T(8,128)}, f32[512,512]{1,0:T(8,128)}), (f32[512,512]{1,0:T(8,128)}, f32[512,512]{1,0:T(8,128)}, f32[512,512]{1,0:T(8,128)})) %all-reduce.3.cloned.1.call-update) | async-done | bytes 3145744 | tf_op jit(solution)/shard_map/psum | solution.py:43
  512.8 3.7 convolution_bitcast_fusion.1
  516.5 4.8 gather_fusion
  523.5 1.0 convolution_subtract_fusion.9
  524.9 1.5 convolution_subtract_fusion.15
  528.2 1.0 convolution_subtract_fusion.7
  529.6 1.5 convolution_subtract_fusion.14
  531.5 1.3 fusion.111
  532.8 0.7 copy-done.13
  533.5 1.0 fusion.42
  534.6 1.6 copy.29
  536.2 3.8 fusion.7
  540.4 1.0 convolution_subtract_fusion.6
  541.8 1.0 convolution_subtract_fusion.5
  543.9 2.2 convolution_subtract_fusion.13
  546.1 1.1 copy.31
  547.1 1.1 copy.32
  548.4 1.5 fusion.123
  549.9 1.0 multiply_bitcast_fusion
  550.9 3.4 fusion.4
  554.3 1.9 convolution_bitcast_fusion
  556.2 4.7 gather_fusion.1
  563.2 1.0 convolution_subtract_fusion.3
  564.6 1.5 convolution_subtract_fusion.12
  567.9 1.0 convolution_subtract_fusion.1
  569.3 1.5 convolution_subtract_fusion.11
  570.8 0.8 copy.35
  571.6 0.8 copy.36
  572.4 0.8 copy.37
  574.4 1.2 fusion.41
  575.6 1.3 copy.38
  576.9 2.1 multiply_bitcast_fusion.1
  579.2 1.8 copy.39
  (116 shorter events, 21.2 us)
Async XLA Ops:
  7.2 233.6 %copy-start = (f32[512,512]{1,0:T(8,128)S(1)}, f32[512,512]{1,0:T(8,128)}, u32[]{:S(2)}) copy-start(f32[512,512]{1,0:T(8,128)} %param.12) | copy-start | bytes 3145732
  7.2 56.4 %all-gather.5.cloned.1.call-start = ((), (), s32[]{:S(2)}) async-start(), calls=%async_computation.4 | async-start | bytes 2228224 | tf_op jit(solution)/shard_map/all_gather | solution.py:35
  9.0 106.9 %all-gather.7.cloned.1.call-start = ((), (), s32[]{:S(2)}) async-start(), calls=%async_computation.5 | async-start | bytes 2228224 | tf_op jit(solution)/shard_map/all_gather | solution.py:35
  9.8 216.6 %reduce-scatter.3.cloned.1.call-start = ((), (), s32[]{:S(2)}) async-start(), calls=%async_computation.2 | async-start | bytes 2228224 | tf_op jit(solution)/shard_map/reduce_scatter | solution.py:36
  73.8 1.6 copy-start.1
  73.8 166.9 %reduce-scatter.5.cloned.1.call-start = ((), (), s32[]{:S(2)}) async-start(), calls=%async_computation.3 | async-start | bytes 2228224 | tf_op jit(solution)/shard_map/reduce_scatter | solution.py:36
  126.1 51.7 %copy-start.3 = (f32[512,512]{1,0:T(8,128)S(1)}, f32[512,512]{1,0:T(8,128)}, u32[]{:S(2)}) copy-start(f32[512,512]{1,0:T(8,128)} %get-tuple-element.169) | copy-start | bytes 3145732
  126.1 100.3 %copy-start.20 = (f32[2,64,512]{2,1,0:T(8,128)S(1)}, f32[2,64,512]{2,1,0:T(8,128)}, u32[]{:S(2)}) copy-start(f32[2,64,512]{2,1,0:T(8,128)} %param.16) | copy-start | bytes 786436
  126.1 105.6 %copy-start.19 = (f32[2,64,512]{2,1,0:T(8,128)S(1)}, f32[2,64,512]{2,1,0:T(8,128)}, u32[]{:S(2)}) copy-start(f32[2,64,512]{2,1,0:T(8,128)} %param.13) | copy-start | bytes 786436
  126.2 386.6 %all-reduce.3.cloned.1.call-start = ((), (), s32[]{:S(2)}) async-start(), calls=%async_computation.6 | async-start | bytes 6291456 | tf_op jit(solution)/shard_map/psum | solution.py:43
  177.8 351.5 %copy-start.15 = (f32[4,128,128]{1,2,0:T(8,128)}, f32[4,128,128]{1,2,0:T(8,128)S(1)}, u32[]{:S(2)}) copy-start(f32[4,128,128]{1,2,0:T(8,128)S(1)} %custom-call.17) | copy-start | bytes 786436
  185.5 0.7 copy-start.21
  226.3 19.8 %copy-start.6 = (f32[4,128,128]{1,2,0:T(8,128)}, f32[4,128,128]{1,2,0:T(8,128)S(1)}, u32[]{:S(2)}) copy-start(f32[4,128,128]{1,2,0:T(8,128)S(1)} %custom-call.21) | copy-start | bytes 786436
  521.3 1.2 copy-start.5
  531.2 4.9 copy-start.9
  531.4 1.4 copy-start.11
  531.5 1.3 copy-start.12
  532.8 0.7 copy-start.13
  536.2 3.8 copy-start.7
  541.8 1.4 copy-start.14
  543.2 0.7 copy-start.16
  548.4 2.6 copy-start.18
  550.9 3.4 copy-start.2
  556.2 4.9 copy-start.8
  561.0 1.2 copy-start.4
  573.7 0.7 copy-start.17
  574.4 2.5 copy-start.10
Sparse Core Ops, SparseCore 0:
  11.0 52.5 all-gather.4
  66.6 49.3 all-gather.6
  119.0 60.2 reduce-scatter.2
  181.7 58.9 reduce-scatter.4
  246.9 265.8 all-reduce.2
where the time goes:
time: 594 us; the launch traced here: 588 us
  waiting for transfers between devices  364 us (61%)
  other arithmetic  88.8 us (15%)
  matrix products  72.9 us (12%)
  local copies, waits for them, and re-layouts  46.4 us (8%)
  between operations  14.8 us (2%)
    psum x1, waiting for transfers between devices, shards(): lax.psum(product(second_solved.T, factor_low[1]), ('row', 'col'))  266 us
    all_gather x2, waiting for transfers between devices, image_of(): columns = lax.all_gather(panel, 'row', axis=0, tiled=True)  92.8 us
    another operation x4, other arithmetic, right_solve(): jax.scipy.linalg.solve_triangular(factor, row_block.T, trans=1, lower=True)  81 us
    dot_general x10, matrix products, product(): jnp.dot(left_side, right_side, precision=lax.Precision.HIGHEST, preferred...  41 us
    another operation x36, local copies, waits for them, and re-layouts, right_solve(): jax.scipy.linalg.solve_triangular(factor, row_block.T, trans=1, lower=True)  24.7 us
    another operation x35, matrix products, right_solve(): jax.scipy.linalg.solve_triangular(factor, row_block.T, trans=1, lower=True)  22.8 us
  transfers between devices with their start and end apart: 5, of which 4 were waited for; matrix products, arithmetic and copies ran while one was open for 22% of the time, Pallas kernels for 0%

commit v1 on v0

--- a/solution.py
+++ b/solution.py
@@ -1,7 +1,16 @@
+import functools
 import jax
 import jax.numpy as jnp
 from jax import lax
 from jax.sharding import PartitionSpec as P
+
+
+def store_the_side(u_in, chip_axis, shard_axis):
+    x_now = jax.lax.psum(jax.lax.psum(u_in, axis_name=chip_axis), axis_name=shard_axis)
+    return x_now
+
+
+classes_watch = functools.partial(store_the_side, chip_axis="col", shard_axis="row")
 
 
 def lower_half(matrix):
@@ -40,7 +49,7 @@
     second_image = image_of(factor_low[1])
     first_image = image_of(factor_low[0])
     second_solved = right_solve(factor_diag[1], adjoint_low[1] - 2.0 * second_image)
-    second_total = lax.psum(product(second_solved.T, factor_low[1]), ("row", "col"))
+    second_total = classes_watch(product(second_solved.T, factor_low[1]))
     second_grad = diag_adjoint(factor_diag[1], adjoint_diag[1] - second_total)
     second_half = 0.5 * second_solved
     upper_term = product(second_half.T, factor_low[0])

time: 594 us -> 789 us (1.33)
  waiting for transfers between devices: 364 us -> 539 us
  matrix products: 72.9 us -> 89.9 us
    psum x1 -> x3, waiting for transfers between devices: 266 us -> 438 us  [the longest x1 233 us: shards(): lower_total = lax.psum(lower_term, ('row', 'col'))]
    another operation x35, matrix products: 22.8 us -> 37.1 us  [right_solve(): jax.scipy.linalg.solve_triangular(factor, row_block.T, trans=1, lower=True)]
  transfers between devices with their start and end apart: 5 -> 7, of which waited for: 4 -> 6; matrix products, arithmetic and copies ran while one was open for 22% -> 22% of each run, Pallas kernels for 0% -> 0%
where the time goes in v1:
time: 789 us; the launch traced here: 782 us
  waiting for transfers between devices  539 us (68%)
  other arithmetic  92.1 us (12%)
  matrix products  89.9 us (11%)
  local copies, waits for them, and re-layouts  45.1 us (6%)
  between operations  15.1 us (2%)
    psum x1, waiting for transfers between devices, shards(): lower_total = lax.psum(lower_term, ('row', 'col'))  233 us
    psum x1, waiting for transfers between devices, store_the_side(): jax.lax.psum(u_in, axis_name=chip_axis)  110 us
    psum x1, waiting for transfers between devices, store_the_side(): jax.lax.psum(jax.lax.psum(u_in, axis_name=chip_axis), axis_name=shard_axis)  95.3 us
    all_gather x2, waiting for transfers between devices, image_of(): columns = lax.all_gather(panel, 'row', axis=0, tiled=True)  92.7 us
    another operation x4, other arithmetic, right_solve(): jax.scipy.linalg.solve_triangular(factor, row_block.T, trans=1, lower=True)  81.1 us
    dot_general x10, matrix products, product(): jnp.dot(left_side, right_side, precision=lax.Precision.HIGHEST, preferred...  41 us
    another operation x35, matrix products, right_solve(): jax.scipy.linalg.solve_triangular(factor, row_block.T, trans=1, lower=True)  37.1 us
    another operation x36, local copies, waits for them, and re-layouts, right_solve(): jax.scipy.linalg.solve_triangular(factor, row_block.T, trans=1, lower=True)  23.1 us
  transfers between devices with their start and end apart: 7, of which 6 were waited for; matrix products, arithmetic and copies ran while one was open for 22% of the time, Pallas kernels for 0%

profile of v1, /device:TPU:2, one launch (start us, length us, event | category | flops | bytes accessed | tf_op | source)
XLA Modules:
  0.0 781.9 jit_solution(8507142945340313736)
XLA Ops:
  7.2 1.8 fusion.165
  9.8 53.8 %all-gather.5.cloned.1.call-done = f32[1,1024,512]{2,1,0:T(8,128)} async-done(((f32[1,64,512]{2,1,0:T(8,128)}), f32[1,1024,512]{2,1,0:T(8,128)}) %all-gather.5.cloned.1.call-update) | async-done | bytes 2097168 | tf_op jit(solution)/shard_map/all_gather | solution.py:44
  63.6 10.2 %fusion.2 = f32[1024,512]{1,0:T(8,128)} fusion(f32[1024,1024]{0,1:T(8,128)} %bitcast.202, f32[1,1024,512]{2,1,0:T(8,128)} %all-gather.5.cloned.1.call-done), kind=kOutput, calls=%fused_computation.9 | convolution fusion | flops 6442450944 | bytes 8388608 | tf_op jit(solution)/shard_map/dot_general | solution.py:21
  73.8 1.5 copy-done.1
  75.3 1.6 bitcast_select_fusion.1
  77.0 39.0 %all-gather.7.cloned.1.call-done = f32[1,1024,512]{2,1,0:T(8,128)} async-done(((f32[1,64,512]{2,1,0:T(8,128)}), f32[1,1024,512]{2,1,0:T(8,128)}) %all-gather.7.cloned.1.call-update) | async-done | bytes 2097168 | tf_op jit(solution)/shard_map/all_gather | solution.py:44
  115.9 10.2 %fusion = f32[1024,512]{1,0:T(8,128)} fusion(f32[1024,1024]{0,1:T(8,128)} %bitcast.203, f32[1,1024,512]{2,1,0:T(8,128)} %all-gather.7.cloned.1.call-done), kind=kOutput, calls=%fused_computation.7 | convolution fusion | flops 6442450944 | bytes 8388608 | tf_op jit(solution)/shard_map/dot_general | solution.py:21
  126.4 11.7 %while.14 = (s32[]{:T(128)}, f32[512,512]{1,0:T(8,128)}, s32[4,2]{0,1:T(2,128)S(1)}, f32[4,128,128]{2,1,0:T(8,128)S(1)}, s32[]{:T(128)}) while((s32[]{:T(128)}, f32[512,512]{1,0:T(8,128)}, s32[4,2]{0,1:T(2,128)S(1)}, f32[4,128,128]{2,1,0:T(8,128)S(1)}, s32[]{:T(128)}) %tuple.60), condition=%wide.while_cond.1.clone, body=%wide.while_body.1.clone.sunk | while | flops 2 | bytes 131189 | solution.py:27
  127.1 2.3 bitcast_dynamic-update-slice_fusion.4
  130.0 2.3 bitcast_dynamic-update-slice_fusion.4
  133.0 2.3 bitcast_dynamic-update-slice_fusion.4
  135.9 2.2 bitcast_dynamic-update-slice_fusion.4
  138.2 39.3 %custom-call.17 = f32[4,128,128]{1,2,0:T(8,128)S(1)} custom-call(f32[4,128,128]{2,1,0:T(8,128)S(1)} %get-tuple-element.53), custom_call_target="InvertDiagBlocksLowerTriangular" | custom-call | tf_op jit(solution)/shard_map/jit(_solve_triangular)/triangular_solve | solution.py:27
  177.5 8.0 %while.15 = (s32[]{:T(128)}, f32[512,512]{1,0:T(8,128)S(1)}, s32[4,2]{0,1:T(2,128)S(1)}, f32[4,128,128]{2,1,0:T(8,128)S(1)}, s32[]{:T(128)}) while((s32[]{:T(128)}, f32[512,512]{1,0:T(8,128)S(1)}, s32[4,2]{0,1:T(2,128)S(1)}, f32[4,128,128]{2,1,0:T(8,128)S(1)}, s32[]{:T(128)}) %tuple.82), condition=%wide.while_cond.1.clone.3, body=%wide.while_body.1.clone.3.sunk | while | flops 2 | bytes 131189 | solution.py:27
  178.1 1.4 bitcast_dynamic-update-slice_fusion.5
  180.1 1.4 bitcast_dynamic-update-slice_fusion.5
  182.1 1.4 bitcast_dynamic-update-slice_fusion.5
  184.1 1.4 bitcast_dynamic-update-slice_fusion.5
  186.2 40.1 %custom-call.21 = f32[4,128,128]{1,2,0:T(8,128)S(1)} custom-call(f32[4,128,128]{2,1,0:T(8,128)} %copy-done.22), custom_call_target="InvertDiagBlocksLowerTriangular" | custom-call | tf_op jit(solution)/shard_map/jit(_solve_triangular)/triangular_solve | solution.py:27
  227.6 1.0 convolution_subtract_fusion.21
  228.9 1.1 convolution_subtract_fusion.20
  230.3 1.2 convolution_subtract_fusion.19
  231.7 2.0 fusion.79
  233.7 7.0 reduce-scatter.5.cloned.1.call-done
  240.8 1.7 fusion.10
  244.0 110.4 %all-reduce.5.cloned.1.call-done = f32[512,512]{1,0:T(8,128)} async-done(((f32[512,512]{1,0:T(8,128)}), f32[512,512]{1,0:T(8,128)}) %all-reduce.5.cloned.1.call-update) | async-done | bytes 1048592 | tf_op jit(solution)/shard_map/psum | solution.py:9
  355.5 2.0 fusion.75
  357.5 2.0 fusion.77
  359.6 95.3 %all-reduce.7.cloned.1.call-done = f32[512,512]{1,0:T(8,128)} async-done(((f32[512,512]{1,0:T(8,128)}), f32[512,512]{1,0:T(8,128)}) %all-reduce.7.cloned.1.call-update) | async-done | bytes 1048592 | tf_op jit(solution)/shard_map/psum | solution.py:9
  454.8 3.7 convolution_bitcast_fusion.1
  458.6 4.8 gather_fusion
  464.7 1.4 convolution_subtract_fusion.10
  466.5 1.9 convolution_subtract_fusion.9
  468.8 2.4 convolution_subtract_fusion.15
  471.6 1.0 maximum_bitcast_fusion
  472.7 1.3 fusion.64
  474.1 1.7 convolution_subtract_fusion.8
  475.8 1.2 fusion.115
  477.2 2.1 convolution_subtract_fusion.7
  479.3 1.9 fusion.112
  481.2 1.1 copy.26
  482.3 2.8 convolution_subtract_fusion.14
  485.1 1.2 fusion.111
  487.1 1.0 fusion.42
  488.1 1.6 copy.29
  489.7 2.4 fusion.162
  492.0 232.8 %all-reduce.9.cloned.1.call-done = (f32[512,512]{1,0:T(8,128)}, f32[512,512]{1,0:T(8,128)}) async-done(((f32[512,512]{1,0:T(8,128)}, f32[512,512]{1,0:T(8,128)}), (f32[512,512]{1,0:T(8,128)}, f32[512,512]{1,0:T(8,128)})) %all-reduce.9.cloned.1.call-update) | async-done | bytes 2097168 | tf_op jit(solution)/shard_map/psum | solution.py:60
  724.8 3.9 fusion.7
  730.2 1.9 convolution_subtract_fusion.6
  733.4 2.0 convolution_subtract_fusion.5
  735.7 3.1 convolution_subtract_fusion.13
  739.0 1.5 fusion.123
  740.5 2.0 multiply_bitcast_fusion
  742.5 3.4 fusion.4
  745.8 1.9 convolution_bitcast_fusion
  747.8 4.7 gather_fusion.1
  755.4 1.5 convolution_subtract_fusion.12
  758.8 1.6 convolution_subtract_fusion.2
  761.7 1.9 convolution_subtract_fusion.1
  764.0 3.1 convolution_subtract_fusion.11
  767.3 1.4 fusion.125
  769.4 1.0 fusion.41
  771.4 1.3 multiply_bitcast_fusion.1
  773.0 1.8 copy.39
  (126 shorter events, 26.3 us)
Async XLA Ops:
  7.2 233.6 %copy-start = (f32[512,512]{1,0:T(8,128)S(1)}, f32[512,512]{1,0:T(8,128)}, u32[]{:S(2)}) copy-start(f32[512,512]{1,0:T(8,128)} %param.12) | copy-start | bytes 3145732
  7.2 56.4 %all-gather.5.cloned.1.call-start = ((), (), s32[]{:S(2)}) async-start(), calls=%async_computation.6 | async-start | bytes 2228224 | tf_op jit(solution)/shard_map/all_gather | solution.py:44
  9.0 106.9 %all-gather.7.cloned.1.call-start = ((), (), s32[]{:S(2)}) async-start(), calls=%async_computation.7 | async-start | bytes 2228224 | tf_op jit(solution)/shard_map/all_gather | solution.py:44
  9.8 216.7 %reduce-scatter.3.cloned.1.call-start = ((), (), s32[]{:S(2)}) async-start(), calls=%async_computation.2 | async-start | bytes 2228224 | tf_op jit(solution)/shard_map/reduce_scatter | solution.py:45
  73.8 1.6 copy-start.1
  73.8 167.0 %reduce-scatter.5.cloned.1.call-start = ((), (), s32[]{:S(2)}) async-start(), calls=%async_computation.5 | async-start | bytes 2228224 | tf_op jit(solution)/shard_map/reduce_scatter | solution.py:45
  126.1 51.4 %copy-start.3 = (f32[512,512]{1,0:T(8,128)S(1)}, f32[512,512]{1,0:T(8,128)}, u32[]{:S(2)}) copy-start(f32[512,512]{1,0:T(8,128)} %get-tuple-element.164) | copy-start | bytes 3145732
  126.1 100.3 %copy-start.21 = (f32[2,64,512]{2,1,0:T(8,128)S(1)}, f32[2,64,512]{2,1,0:T(8,128)}, u32[]{:S(2)}) copy-start(f32[2,64,512]{2,1,0:T(8,128)} %param.16) | copy-start | bytes 786436
  126.1 105.6 %copy-start.20 = (f32[2,64,512]{2,1,0:T(8,128)S(1)}, f32[2,64,512]{2,1,0:T(8,128)}, u32[]{:S(2)}) copy-start(f32[2,64,512]{2,1,0:T(8,128)} %param.13) | copy-start | bytes 786436
  126.1 228.3 %all-reduce.5.cloned.1.call-start = ((), (), s32[]{:S(2)}) async-start(), calls=%async_computation.3 | async-start | bytes 2097152 | tf_op jit(solution)/shard_map/psum | solution.py:9
  177.5 65.0 %copy-start.12 = (f32[4,128,128]{1,2,0:T(8,128)}, f32[4,128,128]{1,2,0:T(8,128)S(1)}, u32[]{:S(2)}) copy-start(f32[4,128,128]{1,2,0:T(8,128)S(1)} %custom-call.17) | copy-start | bytes 786436
  185.5 0.7 copy-start.22
  243.2 211.6 %all-reduce.7.cloned.1.call-start = ((), (), s32[]{:S(2)}) async-start(), calls=%async_computation.4 | async-start | bytes 2097152 | tf_op jit(solution)/shard_map/psum | solution.py:9
  354.4 370.4 %all-reduce.9.cloned.1.call-start = ((), (), s32[]{:S(2)}) async-start(), calls=%async_computation.8 | async-start | bytes 4194304 | tf_op jit(solution)/shard_map/psum | solution.py:60
  463.4 1.0 copy-start.13
  474.1 12.2 %copy-start.6 = (f32[128,512]{0,1:T(8,128)}, f32[128,512]{0,1:T(8,128)S(1)}, u32[]{:S(2)}) copy-start(f32[128,512]{0,1:T(8,128)S(1)} %copy.28) | copy-start | bytes 786436
  477.0 2.3 copy-start.11
  477.2 9.2 %copy-start.7 = (f32[128,512]{0,1:T(8,128)}, f32[128,512]{0,1:T(8,128)S(1)}, u32[]{:S(2)}) copy-start(f32[128,512]{0,1:T(8,128)S(1)} %copy.27) | copy-start | bytes 786436
  482.3 4.0 copy-start.8
  486.4 0.7 copy-start.9
  728.7 1.0 copy-start.10
  738.8 3.6 copy-start.16
  739.0 3.5 copy-start.19
  742.5 3.4 copy-start.2
  757.3 1.0 copy-start.5
  758.8 9.9 %copy-start.14 = (f32[128,512]{0,1:T(8,128)}, f32[128,512]{0,1:T(8,128)S(1)}, u32[]{:S(2)}) copy-start(f32[128,512]{0,1:T(8,128)S(1)} %copy.37) | copy-start | bytes 786436
  767.3 1.5 copy-start.17
  768.7 0.7 copy-start.18
  770.5 1.0 copy-start.15
  771.4 1.5 copy-start.4
Sparse Core Ops, SparseCore 0:
  11.0 52.5 all-gather.4
  66.6 49.3 all-gather.6
  119.0 60.2 reduce-scatter.2
  181.7 59.0 reduce-scatter.4
  243.5 110.8 all-reduce.4
  357.5 97.2 all-reduce.6
  460.4 264.3 all-reduce.8
